TPU v7x, 32 devices: a whole 2x2x4 slice. The times are simulated.
32 devices in a mesh: sec: 4 (over y, x), ctx: 2 (over core), ch: 4 (over z).
Axes of the slice: x: 2, y: 2, z: 4, core: 2. Of those that a mesh axis runs over, the one named last changes fastest.
Arguments:
- inputs: bfloat16 [256, 4096], P('ctx', ('ch', 'sec')), may hold values from -2500 to 2500, as said below
- query_fields: bfloat16 [4, 256, 4096], P('sec', 'ctx', 'ch'), may hold values from -3 to 3
- key_fields: bfloat16 [4, 256, 4096], P('sec', 'ctx', 'ch'), may hold values from -4 to 4
- norm_gain: float32 [4096], P('ch'), may hold values from 0.1 to 1.9
- short_taps: float32 [2, 7, 4096], P(None, None, 'ch'), may hold values from -2 to 2
- medium_taps: float32 [128, 4096], P(None, 'ch'), may hold values from -0.5 to 0.5
- pole_rates: float32 [8, 4096], P(None, 'ch'), as said below
- pole_residues: float32 [8, 4096], P(None, 'ch'), may hold values from -2 to 2
- direct_term: float32 [4096], P('ch'), may hold values from -3 to 3
Outputs:
- mixed_stream: bfloat16 [256, 4096], P('ctx', ('ch', 'sec'))
Inputs may be any that keep to these rules, and one draw needn't show every extreme that they name: `inputs`: scaled real values. `pole_rates`: Positive, from 0.2 / 256 to 1 / 30.
All inputs are finite; a program needn't handle non-finite values.
Results may differ from a plain program's by a relative error of at most 0.013.
Values may be sent and summed in bfloat16 or wider, within the bound.
A program may use at most 64 MiB of HBM per device.

v0:
```python
import functools

import jax
import jax.numpy as jnp
from jax import lax
from jax.experimental import pallas as pl
from jax.experimental.pallas import tpu as pltpu
from jax.sharding import PartitionSpec as P

norm_eps = 1e-06
MESH = pl.DeviceIdType.MESH
LANES = 128
ROWS = 8
F32 = jnp.float32


def row_ids(shape):
    return lax.broadcasted_iota(jnp.int32, shape, 0)


def shifted(values, steps):
    if steps == 0:
        return values, jnp.zeros((ROWS, values.shape[1]), F32)
    moved = pltpu.roll(values, steps, 0)
    top = moved[:ROWS]
    inside = row_ids(top.shape) >= steps
    first = jnp.where(inside, top, 0.0)
    if values.shape[0] > ROWS:
        first = jnp.concatenate([first, moved[ROWS:]], axis=0)
    return first, jnp.where(inside, 0.0, top)


def filter_within(values, taps):
    length = values.shape[0]
    span = taps.shape[0]
    total = jnp.zeros(values.shape, F32)
    for step in range(min(ROWS, span)):
        moved, _ = shifted(values, step)
        for tap in range(step, min(span, length), ROWS):
            base = tap - step
            part = moved[: length - base] * taps[tap : tap + 1]
            if base:
                total = jnp.concatenate([total[:base], total[base:] + part], axis=0)
            else:
                total = total + part
    return total


def filter_before(history, taps, length, own=0):
    span = taps.shape[0]
    known = history.shape[0] - own
    total = jnp.zeros((length, history.shape[1]), F32)
    for step in range(min(ROWS, span)):
        moved, fallen = shifted(history, step)
        joined = jnp.concatenate([moved, fallen], axis=0)
        for tap in range(step, span, ROWS):
            base = tap - step
            reach = min(base + ROWS + own, length)
            part = joined[known - base : known - base + reach] * taps[tap : tap + 1]
            if reach < length:
                total = jnp.concatenate([total[:reach] + part, total[reach:]], axis=0)
            else:
                total = total + part
    return total


def kernel(
    sections,
    n_ctx,
    n_ch,
    inputs,
    query,
    key,
    gain,
    short,
    medium,
    rates,
    residues,
    direct,
    out,
    x_ref,
    gain_ref,
    short_ref,
    medium_ref,
    rate_ref,
    residue_ref,
    direct_ref,
    key_ref,
    query_ref,
    sums_sec,
    sums_ch,
    gated_ref,
    filtered_ref,
    stream_ref,
    tail_ref,
    rows_ref,
    state_ref,
    leaving_ref,
    taps_ref,
    age_ref,
    carry_ref,
    top_ref,
    load_sem,
    key_send,
    key_recv,
    query_send,
    query_recv,
    sec_send,
    sec_recv,
    ch_send,
    ch_recv,
    ctx_send,
    ctx_recv,
):
    length, width = x_ref.shape
    modes = rate_ref.shape[0]
    sec = lax.axis_index("sec")
    ctx = lax.axis_index("ctx")
    ch = lax.axis_index("ch")
    has_before = ctx > 0
    has_after = ctx < n_ctx - 1

    def cut(index):
        return pl.ds(pl.multiple_of(index * width, width), width)

    mine = cut(sec)
    loads = [
        pltpu.make_async_copy(inputs, x_ref, load_sem.at[0]),
        pltpu.make_async_copy(rates.at[:, mine], rate_ref, load_sem.at[1]),
        pltpu.make_async_copy(residues.at[:, mine], residue_ref, load_sem.at[2]),
        pltpu.make_async_copy(direct.at[:, mine], direct_ref, load_sem.at[3]),
        pltpu.make_async_copy(gain.at[:, mine], gain_ref, load_sem.at[4]),
        pltpu.make_async_copy(short.at[:, :, mine], short_ref, load_sem.at[5]),
        pltpu.make_async_copy(medium.at[:, mine], medium_ref, load_sem.at[6]),
        pltpu.make_async_copy(key.at[0, :, mine], key_ref.at[sec], key_recv.at[sec]),
        pltpu.make_async_copy(query.at[0, :, mine], query_ref.at[sec], query_recv.at[sec]),
    ]
    for load in loads:
        load.start()

    sec_peers = [lax.rem(sec + step, sections) for step in range(1, sections)]
    ch_peers = [lax.rem(ch + step, n_ch) for step in range(1, n_ch)]
    barrier = pltpu.get_barrier_semaphore()
    for peer in sec_peers:
        pl.semaphore_signal(barrier, inc=1, device_id={"sec": peer}, device_id_type=MESH)
    for peer in ch_peers:
        pl.semaphore_signal(barrier, inc=1, device_id={"ch": peer}, device_id_type=MESH)

    @pl.when(has_before)
    def _():
        pl.semaphore_signal(barrier, inc=1, device_id={"ctx": ctx - 1}, device_id_type=MESH)

    @pl.when(has_after)
    def _():
        pl.semaphore_signal(barrier, inc=1, device_id={"ctx": ctx + 1}, device_id_type=MESH)

    loads[0].wait()
    squares = jnp.square(x_ref[...].astype(F32))
    folded = sum(squares[:, low : low + LANES] for low in range(0, width, LANES))
    partial = jnp.sum(folded.T, axis=0, keepdims=True)
    sums_sec[sec] = partial

    around = has_before.astype(jnp.int32) + has_after.astype(jnp.int32)
    pl.semaphore_wait(barrier, len(sec_peers) + len(ch_peers) + around)

    def remote(src, dst, send_sem, recv_sem, device):
        return pltpu.make_async_remote_copy(
            src_ref=src,
            dst_ref=dst,
            send_sem=send_sem,
            recv_sem=recv_sem,
            device_id=device,
            device_id_type=MESH,
        )

    sends = []
    for step, peer in enumerate(sec_peers):
        slot = sums_sec.at[sec]
        sends.append(remote(slot, slot, sec_send.at[step], sec_recv.at[sec], {"sec": peer}))
    for field, held, send_sem, recv_sem in (
        (key, key_ref, key_send, key_recv),
        (query, query_ref, query_send, query_recv),
    ):
        for step, peer in enumerate(sec_peers):
            sends.append(
                remote(
                    field.at[0, :, cut(peer)],
                    held.at[sec],
                    send_sem.at[step],
                    recv_sem.at[sec],
                    {"sec": peer},
                )
            )
    for send in sends:
        send.start()

    def arrived(ref, sem):
        pltpu.make_async_copy(ref, ref, sem).wait()

    for load in loads[1:4]:
        load.wait()
    offsets = row_ids((length, width)).astype(F32)
    rate_table = rate_ref[...]
    weights = residue_ref[...] * jnp.sqrt(1.0 - jnp.exp(-2.0 * rate_table))
    taps = jnp.where(row_ids((length, width)) == 0, direct_ref[...], 0.0)
    for mode in range(modes):
        part = weights[mode : mode + 1] * jnp.exp(-rate_table[mode : mode + 1] * offsets)
        carry_ref[mode] = part
        taps = taps + part
    taps_ref[...] = taps

    for peer in sec_peers:
        arrived(sums_sec.at[peer], sec_recv.at[peer])
    total = sums_sec[0]
    for index in range(1, sections):
        total = total + sums_sec[index]
    sums_ch[ch] = total
    for step, peer in enumerate(ch_peers):
        slot = sums_ch.at[ch]
        send = remote(slot, slot, ch_send.at[step], ch_recv.at[ch], {"ch": peer})
        send.start()
        sends.append(send)

    @pl.when(has_after)
    def _():
        ages = (length - 1.0) - offsets
        for mode in range(modes):
            age_ref[mode] = jnp.exp(-rate_table[mode : mode + 1] * ages)

    for load in loads[4:7]:
        load.wait()

    for peer in ch_peers:
        arrived(sums_ch.at[peer], ch_recv.at[peer])
    total = sums_ch[0]
    for index in range(1, n_ch):
        total = total + sums_ch[index]
    inverse = lax.rsqrt(total / (width * sections * n_ch) + norm_eps)
    scale = jnp.broadcast_to(inverse[:1], (length, length)).T[:, :1]
    stream = x_ref[...].astype(F32) * scale * gain_ref[...]
    stream_ref[...] = stream.astype(jnp.bfloat16).astype(F32)

    halves = [slice(low, low + LANES) for low in range(0, width, LANES)]
    after = {"ctx": lax.rem(ctx + 1, n_ctx)}

    def short_section(section, tap_set, tail_slot):
        hand = remote(
            gated_ref.at[section, pl.ds(length - ROWS, ROWS)],
            tail_ref.at[tail_slot],
            ctx_send.at[section],
            ctx_recv.at[section],
            after,
        )

        @pl.when(has_after)
        def _():
            hand.start()

        for half in halves:
            filtered_ref[:, half] = filter_within(
                gated_ref[section, :, half], short_ref[:, tap_set, half]
            )

        if section:

            @pl.when(has_before)
            def _():
                hand.wait_recv()
                finish_top(tail_slot, tap_set)

        return hand

    def finish_top(tail_slot, tap_set):
        for half in halves:
            filtered_ref[:ROWS, half] += filter_before(
                tail_ref[tail_slot, :, half], short_ref[:, tap_set, half], ROWS
            )

    def medium_section(section, earlier):
        @pl.when(has_before)
        def _():
            gated_ref[section, :ROWS] = jnp.zeros((ROWS, width), F32)

        hand = remote(
            gated_ref.at[section], rows_ref, ctx_send.at[section], ctx_recv.at[section], after
        )

        @pl.when(jnp.logical_and(has_after, jnp.logical_not(has_before)))
        def _():
            hand.start()

        for half in halves:
            filtered_ref[:, half] = filter_within(
                gated_ref[section, :, half], medium_ref[:, half]
            )

        @pl.when(has_before)
        def _():
            earlier.wait_recv()
            for half in halves:
                added = filter_before(tail_ref[0, :, half], short_ref[:, 0, half], ROWS)
                gate = query_ref[section - 1, :ROWS, half].astype(F32)
                top = top_ref[0, :, half] + gate * (top_ref[1, :, half] + added)
                top = top.astype(jnp.bfloat16).astype(F32)
                stream_ref[:ROWS, half] = top
                gated_ref[section, :ROWS, half] = key_ref[section, :ROWS, half].astype(F32) * top

        @pl.when(jnp.logical_and(has_after, has_before))
        def _():
            hand.start()

        @pl.when(has_before)
        def _():
            hand.wait_recv()
            for half in halves:
                history = jnp.concatenate(
                    [rows_ref[:, half], gated_ref[section, :ROWS, half]], axis=0
                )
                filtered_ref[:, half] += filter_before(
                    history, medium_ref[:, half], length, ROWS
                )

        return hand

    def long_section(section):
        hand = remote(leaving_ref, state_ref, ctx_send.at[section], ctx_recv.at[section], after)

        @pl.when(has_after)
        def _():
            for mode in range(modes):
                leaving_ref[mode : mode + 1] = jnp.sum(
                    age_ref[mode] * gated_ref[section], axis=0, keepdims=True
                )

        @pl.when(jnp.logical_and(has_after, jnp.logical_not(has_before)))
        def _():
            hand.start()

        @pl.when(has_before)
        def _():
            hand.wait_recv()

        @pl.when(jnp.logical_and(has_after, has_before))
        def _():
            leaving_ref[...] += jnp.exp(-length * rate_ref[...]) * state_ref[...]
            hand.start()

        for half in halves:
            filtered_ref[:, half] = filter_within(gated_ref[section, :, half], taps_ref[:, half])

        @pl.when(has_before)
        def _():
            entering = jnp.exp(-rate_ref[...]) * state_ref[...]
            for half in halves:
                carried = filtered_ref[:, half]
                for mode in range(modes):
                    carried = carried + carry_ref[mode, :, half] * entering[mode : mode + 1, half]
                filtered_ref[:, half] = carried

        return hand

    hands = []
    for section in range(sections):
        arrived(key_ref.at[section], key_recv.at[section])
        gated_ref[section] = key_ref[section].astype(F32) * stream_ref[...]
        if section == 1:
            hands.append(medium_section(section, hands[0]))
        elif section == 2:
            hands.append(long_section(section))
        else:
            hands.append(short_section(section, min(section, 1), min(section, 1)))
        arrived(query_ref.at[section], query_recv.at[section])
        if section == 0:
            top_ref[0] = stream_ref[:ROWS]
            top_ref[1] = filtered_ref[:ROWS]
        stream = stream_ref[...] + query_ref[section].astype(F32) * filtered_ref[...]
        if section == sections - 1:
            out[...] = stream.astype(jnp.bfloat16)
        else:
            stream_ref[...] = stream.astype(jnp.bfloat16).astype(F32)

    for send in sends:
        send.wait_send()

    @pl.when(has_after)
    def _():
        for hand in hands:
            hand.wait_send()


def shards(
    inputs,
    query_fields,
    key_fields,
    norm_gain,
    short_taps,
    medium_taps,
    pole_rates,
    pole_residues,
    direct_term,
):
    sections = lax.axis_size("sec")
    n_ctx = lax.axis_size("ctx")
    n_ch = lax.axis_size("ch")
    length, width = inputs.shape
    modes = pole_rates.shape[0]
    shorts, short_span = short_taps.shape[:2]
    hbm = pl.BlockSpec(memory_space=pltpu.HBM)
    anywhere = pl.BlockSpec(memory_space=pl.ANY)
    dma = pltpu.SemaphoreType.DMA
    return pl.pallas_call(
        functools.partial(kernel, sections, n_ctx, n_ch),
        out_shape=jax.ShapeDtypeStruct((length, width), inputs.dtype),
        in_specs=[anywhere] * 9,
        out_specs=pl.BlockSpec(memory_space=pltpu.VMEM),
        scratch_shapes=[
            pltpu.VMEM((length, width), inputs.dtype),
            pltpu.VMEM((1, width), F32),
            pltpu.VMEM((short_span, shorts, width), F32),
            pltpu.VMEM((medium_taps.shape[0], width), F32),
            pltpu.VMEM((modes, width), F32),
            pltpu.VMEM((modes, width), F32),
            pltpu.VMEM((1, width), F32),
            pltpu.VMEM((sections, length, width), key_fields.dtype),
            pltpu.VMEM((sections, length, width), query_fields.dtype),
            pltpu.VMEM((sections, 1, length), F32),
            pltpu.VMEM((n_ch, 1, length), F32),
            pltpu.VMEM((sections, length, width), F32),
            pltpu.VMEM((length, width), F32),
            pltpu.VMEM((length, width), F32),
            pltpu.VMEM((2, ROWS, width), F32),
            pltpu.VMEM((length, width), F32),
            pltpu.VMEM((modes, width), F32),
            pltpu.VMEM((modes, width), F32),
            pltpu.VMEM((length, width), F32),
            pltpu.VMEM((modes, length, width), F32),
            pltpu.VMEM((modes, length, width), F32),
            pltpu.VMEM((2, ROWS, width), F32),
            dma((7,)),
            dma((sections - 1,)),
            dma((sections,)),
            dma((sections - 1,)),
            dma((sections,)),
            dma((sections - 1,)),
            dma((sections,)),
            dma((n_ch - 1,)),
            dma((n_ch,)),
            dma((sections,)),
            dma((sections,)),
        ],
        compiler_params=pltpu.CompilerParams(collective_id=0, has_side_effects=True),
    )(
        inputs,
        query_fields,
        key_fields,
        norm_gain[None],
        jnp.swapaxes(short_taps, 0, 1),
        medium_taps,
        pole_rates,
        pole_residues,
        direct_term[None],
    )


def solution(mesh):
    in_specs = (
        P("ctx", ("ch", "sec")),
        P("sec", "ctx", "ch"),
        P("sec", "ctx", "ch"),
        P("ch"),
        P(None, None, "ch"),
        P(None, "ch"),
        P(None, "ch"),
        P(None, "ch"),
        P("ch"),
    )
    out_specs = P("ctx", ("ch", "sec"))
    return jax.shard_map(shards, mesh=mesh, in_specs=in_specs, out_specs=out_specs, check_vma=False)
```

profile of v0, /device:TPU:1, one launch (start us, length us, event | category | flops | bytes accessed | tf_op | source)
XLA Modules:
  0.0 17.4 jit_solution(1531899416527225132)
XLA Ops:
  0.0 15.9 %shard_map.91 = bf16[128,256]{1,0:T(8,128)(2,1)} custom-call(bf16[128,256]{1,0:T(8,128)(2,1)} %inputs.1, bf16[1,128,1024]{2,1,0:T(8,128)(2,1)} %query.1, bf16[1,128,1024]{2,1,0:T(8,128)(2,1)} %key.1, f32[1,1024]{1,0:T(1,128)} %bitcast.4, f32[7,2,1024]{2,1,0:T(2,128)} %bitcast.3, f32[128,1024]{1,0:T(8,128)} %medium.1, f32[8,1024]{1,0:T(8,128)} %rates.1, ...), custom_call_target="tpu_custom_call" | custom-call | tf_op jit(solution)/shard_map/pallas_call | solution.py:411
  15.9 1.5 %copy.11 = bf16[128,256]{1,0:T(8,128)(2,1)} copy(bf16[128,256]{1,0:T(8,128)(2,1)} %shard_map.91) | data formatting | bytes 131072
where the time goes:
time: 17.6 us; the launch traced here: 17.4 us
  Pallas kernels  15.9 us (90%)
  local copies, waits for them, and re-layouts  1.47 us (8%)
    pallas_call x1, Pallas kernels, shards(): pl.pallas_call(functools.partial(kernel, sections, n_ctx, n_ch), out_shap...  15.9 us
    unnamed x1, local copies, waits for them, and re-layouts  1.47 us

commit v1 on v0

--- a/solution.py
+++ b/solution.py
@@ -448,8 +448,8 @@
             dma((sections,)),
             dma((sections,)),
         ],
-        compiler_params=pltpu.CompilerParams(collective_id=0, has_side_effects=True),
-    )(
+        compiler_params=pltpu.CompilerParams(collective_id=0, has_side_effects=True, vmem_limit_bytes=8*2**20),
+    )(*[pltpu.with_memory_space_constraint(a, pltpu.HBM) for a in (
         inputs,
         query_fields,
         key_fields,
@@ -459,7 +459,7 @@
         pole_rates,
         pole_residues,
         direct_term[None],
-    )
+    )])
 
 
 def solution(mesh):

time: 17.6 us -> 16.1 us (0.915)
  local copies, waits for them, and re-layouts: 1.47 us -> 0.63 us
  Pallas kernels: 15.9 us -> 15.3 us
    unnamed x1, local copies, waits for them, and re-layouts: 1.47 us -> 0.63 us
    pallas_call x1, Pallas kernels: 15.9 us -> 15.3 us  [shards(): pl.pallas_call(functools.partial(kernel, sections, n_ctx, n_ch), out_shap...]
where the time goes in v1:
time: 16.1 us; the launch traced here: 16 us
  Pallas kernels  15.3 us (95%)
  local copies, waits for them, and re-layouts  0.63 us (4%)
    pallas_call x1, Pallas kernels, shards(): pl.pallas_call(functools.partial(kernel, sections, n_ctx, n_ch), out_shap...  15.3 us
    unnamed x1, local copies, waits for them, and re-layouts  0.63 us

profile of v1, /device:TPU:1, one launch (start us, length us, event | category | flops | bytes accessed | tf_op | source)
XLA Modules:
  0.0 16.0 jit_solution(1781018092026205806)
XLA Ops:
  0.0 15.3 %shard_map.91 = bf16[128,256]{1,0:T(8,128)(2,1)S(1)} custom-call(bf16[128,256]{1,0:T(8,128)(2,1)} %inputs.1, bf16[1,128,1024]{2,1,0:T(8,128)(2,1)} %query.1, bf16[1,128,1024]{2,1,0:T(8,128)(2,1)} %key.1, f32[1,1024]{1,0:T(1,128)} %bitcast.4, f32[7,2,1024]{2,1,0:T(2,128)} %bitcast.3, f32[128,1024]{1,0:T(8,128)} %medium.1, f32[8,1024]{1,0:T(8,128)} %rates.1, ...), custom_call_target="tpu_custom_call" | custom-call | tf_op jit(solution)/shard_map/pallas_call | solution.py:411
  15.3 0.6 %copy.11 = bf16[128,256]{1,0:T(8,128)(2,1)} copy(bf16[128,256]{1,0:T(8,128)(2,1)S(1)} %shard_map.91) | data formatting | bytes 131072

commit v2 on v1

--- a/solution.py
+++ b/solution.py
@@ -87,8 +87,7 @@
     direct_ref,
     key_ref,
     query_ref,
-    sums_sec,
-    sums_ch,
+    sums_ref,
     gated_ref,
     filtered_ref,
     stream_ref,
@@ -105,12 +104,12 @@
     key_recv,
     query_send,
     query_recv,
-    sec_send,
-    sec_recv,
-    ch_send,
-    ch_recv,
+    sum_send,
+    sum_recv,
     ctx_send,
     ctx_recv,
+    down_sem,
+    ready_sem,
 ):
     length, width = x_ref.shape
     modes = rate_ref.shape[0]
@@ -139,29 +138,37 @@
         load.start()
 
     sec_peers = [lax.rem(sec + step, sections) for step in range(1, sections)]
-    ch_peers = [lax.rem(ch + step, n_ch) for step in range(1, n_ch)]
     barrier = pltpu.get_barrier_semaphore()
+
+    def signal(near, sem, device):
+        @pl.when(near)
+        def _():
+            pl.semaphore_signal(sem, inc=1, device_id=device, device_id_type=MESH)
+
+    everyone = [lax.rem(sec + step, sections) for step in range(sections)]
+
+    def planes(ahead):
+        for step in range(1, n_ch):
+            plane = ch + ahead * step
+            yield plane, plane < n_ch if ahead > 0 else plane >= 0
+
+    def signal_planes(sem, ahead):
+        for plane, inside in planes(ahead):
+
+            @pl.when(inside)
+            def _(plane=plane):
+                for peer in everyone:
+                    pl.semaphore_signal(
+                        sem, inc=1, device_id={"sec": peer, "ch": plane}, device_id_type=MESH
+                    )
+
     for peer in sec_peers:
         pl.semaphore_signal(barrier, inc=1, device_id={"sec": peer}, device_id_type=MESH)
-    for peer in ch_peers:
-        pl.semaphore_signal(barrier, inc=1, device_id={"ch": peer}, device_id_type=MESH)
-
-    @pl.when(has_before)
-    def _():
-        pl.semaphore_signal(barrier, inc=1, device_id={"ctx": ctx - 1}, device_id_type=MESH)
-
-    @pl.when(has_after)
-    def _():
-        pl.semaphore_signal(barrier, inc=1, device_id={"ctx": ctx + 1}, device_id_type=MESH)
-
-    loads[0].wait()
-    squares = jnp.square(x_ref[...].astype(F32))
-    folded = sum(squares[:, low : low + LANES] for low in range(0, width, LANES))
-    partial = jnp.sum(folded.T, axis=0, keepdims=True)
-    sums_sec[sec] = partial
-
-    around = has_before.astype(jnp.int32) + has_after.astype(jnp.int32)
-    pl.semaphore_wait(barrier, len(sec_peers) + len(ch_peers) + around)
+    signal(has_after, barrier, {"ctx": ctx + 1})
+    signal_planes(barrier, 1)
+    pl.semaphore_wait(barrier, len(sec_peers) + has_before.astype(jnp.int32) + sections * ch)
+    signal(has_before, ready_sem, {"ctx": ctx - 1})
+    signal_planes(down_sem, -1)
 
     def remote(src, dst, send_sem, recv_sem, device):
         return pltpu.make_async_remote_copy(
@@ -173,10 +180,21 @@
             device_id_type=MESH,
         )
 
-    sends = []
-    for step, peer in enumerate(sec_peers):
-        slot = sums_sec.at[sec]
-        sends.append(remote(slot, slot, sec_send.at[step], sec_recv.at[sec], {"sec": peer}))
+    own = ch * sections + sec
+
+    def sum_copy(to_sec, to_ch):
+        slot = sums_ref.at[own]
+        place = to_ch * sections + to_sec
+        return remote(
+            slot, slot, sum_send.at[place], sum_recv.at[own], {"sec": to_sec, "ch": to_ch}
+        )
+
+    loads[0].wait()
+    squares = jnp.square(x_ref[...].astype(F32))
+    folded = sum(squares[:, low : low + LANES] for low in range(0, width, LANES))
+    sums_ref[own] = jnp.sum(folded.T, axis=0, keepdims=True)
+
+    sends = [sum_copy(peer, ch) for peer in sec_peers]
     for field, held, send_sem, recv_sem in (
         (key, key_ref, key_send, key_recv),
         (query, query_ref, query_send, query_recv),
@@ -191,8 +209,25 @@
                     {"sec": peer},
                 )
             )
-    for send in sends:
+    def send_sums(ahead):
+        for plane, inside in planes(ahead):
+
+            @pl.when(inside)
+            def _(plane=plane):
+                for peer in everyone:
+                    sum_copy(peer, plane).start()
+
+    for send in sends[: len(sec_peers)]:
         send.start()
+    send_sums(-1)
+    for send in sends[len(sec_peers) :]:
+        send.start()
+
+    @pl.when(ch < n_ch - 1)
+    def _():
+        pl.semaphore_wait(down_sem, sections * (n_ch - 1 - ch))
+
+    send_sums(1)
 
     def arrived(ref, sem):
         pltpu.make_async_copy(ref, ref, sem).wait()
@@ -209,18 +244,6 @@
         taps = taps + part
     taps_ref[...] = taps
 
-    for peer in sec_peers:
-        arrived(sums_sec.at[peer], sec_recv.at[peer])
-    total = sums_sec[0]
-    for index in range(1, sections):
-        total = total + sums_sec[index]
-    sums_ch[ch] = total
-    for step, peer in enumerate(ch_peers):
-        slot = sums_ch.at[ch]
-        send = remote(slot, slot, ch_send.at[step], ch_recv.at[ch], {"ch": peer})
-        send.start()
-        sends.append(send)
-
     @pl.when(has_after)
     def _():
         ages = (length - 1.0) - offsets
@@ -230,15 +253,25 @@
     for load in loads[4:7]:
         load.wait()
 
-    for peer in ch_peers:
-        arrived(sums_ch.at[peer], ch_recv.at[peer])
-    total = sums_ch[0]
-    for index in range(1, n_ch):
-        total = total + sums_ch[index]
+    others = [
+        (peer, lax.rem(ch + step, n_ch))
+        for step in range(n_ch)
+        for peer in (everyone if step else sec_peers)
+    ]
+    for from_sec, from_ch in others:
+        place = from_ch * sections + from_sec
+        arrived(sums_ref.at[place], sum_recv.at[place])
+    total = sums_ref[0]
+    for index in range(1, sections * n_ch):
+        total = total + sums_ref[index]
     inverse = lax.rsqrt(total / (width * sections * n_ch) + norm_eps)
     scale = jnp.broadcast_to(inverse[:1], (length, length)).T[:, :1]
     stream = x_ref[...].astype(F32) * scale * gain_ref[...]
     stream_ref[...] = stream.astype(jnp.bfloat16).astype(F32)
+
+    @pl.when(has_after)
+    def _():
+        pl.semaphore_wait(ready_sem, 1)
 
     halves = [slice(low, low + LANES) for low in range(0, width, LANES)]
     after = {"ctx": lax.rem(ctx + 1, n_ctx)}
@@ -381,6 +414,8 @@
 
     for send in sends:
         send.wait_send()
+    for to_sec, to_ch in others[len(sec_peers) :]:
+        sum_copy(to_sec, to_ch).wait_send()
 
     @pl.when(has_after)
     def _():
@@ -423,8 +458,7 @@
             pltpu.VMEM((1, width), F32),
             pltpu.VMEM((sections, length, width), key_fields.dtype),
             pltpu.VMEM((sections, length, width), query_fields.dtype),
-            pltpu.VMEM((sections, 1, length), F32),
-            pltpu.VMEM((n_ch, 1, length), F32),
+            pltpu.VMEM((n_ch * sections, 1, length), F32),
             pltpu.VMEM((sections, length, width), F32),
             pltpu.VMEM((length, width), F32),
             pltpu.VMEM((length, width), F32),
@@ -441,12 +475,12 @@
             dma((sections,)),
             dma((sections - 1,)),
             dma((sections,)),
-            dma((sections - 1,)),
-            dma((sections,)),
-            dma((n_ch - 1,)),
-            dma((n_ch,)),
+            dma((n_ch * sections,)),
+            dma((n_ch * sections,)),
             dma((sections,)),
             dma((sections,)),
+            pltpu.SemaphoreType.REGULAR,
+            pltpu.SemaphoreType.REGULAR,
         ],
         compiler_params=pltpu.CompilerParams(collective_id=0, has_side_effects=True, vmem_limit_bytes=8*2**20),
     )(*[pltpu.with_memory_space_constraint(a, pltpu.HBM) for a in (

time: 16.1 us -> 15.1 us (0.938)
  the two profiles are of different devices: /device:TPU:1 before, /device:TPU:9 now
where the time goes in v2:
time: 15.1 us; the launch traced here: 14.9 us
  Pallas kernels  14.3 us (95%)
  local copies, waits for them, and re-layouts  0.63 us (4%)
    pallas_call x1, Pallas kernels, shards(): pl.pallas_call(functools.partial(kernel, sections, n_ctx, n_ch), out_shap...  14.3 us
    unnamed x1, local copies, waits for them, and re-layouts  0.63 us

profile of v2, /device:TPU:9, one launch (start us, length us, event | category | flops | bytes accessed | tf_op | source)
XLA Modules:
  0.0 14.9 jit_solution(10835508243019286502)
XLA Ops:
  0.0 14.3 %shard_map.91 = bf16[128,256]{1,0:T(8,128)(2,1)S(1)} custom-call(bf16[128,256]{1,0:T(8,128)(2,1)} %inputs.1, bf16[1,128,1024]{2,1,0:T(8,128)(2,1)} %query.1, bf16[1,128,1024]{2,1,0:T(8,128)(2,1)} %key.1, f32[1,1024]{1,0:T(1,128)} %bitcast.4, f32[7,2,1024]{2,1,0:T(2,128)} %bitcast.3, f32[128,1024]{1,0:T(8,128)} %medium.1, f32[8,1024]{1,0:T(8,128)} %rates.1, ...), custom_call_target="tpu_custom_call" | custom-call | tf_op jit(solution)/shard_map/pallas_call | solution.py:446
  14.3 0.6 %copy.11 = bf16[128,256]{1,0:T(8,128)(2,1)} copy(bf16[128,256]{1,0:T(8,128)(2,1)S(1)} %shard_map.91) | data formatting | bytes 131072

commit v3 on v2

v3 whole, which is shorter than its diff:
```python
import functools

import jax
import jax.numpy as jnp
import numpy as np
from jax import lax
from jax.experimental import pallas as pl
from jax.experimental.pallas import tpu as pltpu
from jax.sharding import PartitionSpec as P

norm_eps = 1e-06
MESH = pl.DeviceIdType.MESH
LANES = 128
ROWS = 8
F32 = jnp.float32
BF16 = jnp.bfloat16


def row_ids(shape):
    return lax.broadcasted_iota(jnp.int32, shape, 0)


def parts(values):
    high = values.astype(BF16)
    return high, (values - high.astype(F32)).astype(BF16)


def times(table, values):
    return jnp.dot(table, values.astype(BF16), preferred_element_type=F32)


def times_parts(table, values):
    high, low = parts(values)
    return times(table[0], high) + times(table[0], low) + times(table[1], high)


def waves(length):
    size = 2 * length
    order = np.arange(length)
    turn = 2 * np.pi * np.outer(order, np.arange(size)) / size
    ends = np.cos(np.pi * np.arange(size))
    real, imag = np.cos(turn), -np.sin(turn)
    imag[0] = ends
    back_real, back_imag = 2 * real.T / size, 2 * imag.T / size
    back_real[:, 0] /= 2
    back_imag[:, 0] /= 2
    ahead = np.concatenate([real, imag], axis=0)
    back = np.concatenate([back_real, back_imag], axis=1)[:length]
    own = ahead[:, :length]
    high = own.astype(BF16)
    low = (own - high.astype(np.float64)).astype(BF16)
    return np.stack([high, low]), ahead.astype(BF16), back.astype(BF16)


def kernel(
    sections,
    n_ctx,
    n_ch,
    inputs,
    query,
    key,
    gain,
    short,
    medium,
    rates,
    residues,
    direct,
    own_waves,
    all_waves,
    back_waves,
    out,
    x_ref,
    gain_ref,
    short_ref,
    medium_ref,
    rate_ref,
    residue_ref,
    direct_ref,
    key_ref,
    query_ref,
    sums_ref,
    padded_ref,
    gated_ref,
    rows_ref,
    scaled_ref,
    stream_ref,
    state_ref,
    leaving_ref,
    age_ref,
    carry_ref,
    own_ref,
    all_ref,
    back_ref,
    spectra_ref,
    load_sem,
    key_send,
    key_recv,
    query_send,
    query_recv,
    sum_send,
    sum_recv,
    ctx_send,
    ctx_recv,
    peer_sem,
    far_sem,
    ready_sem,
):
    length, width = x_ref.shape
    modes = rate_ref.shape[0]
    sec = lax.axis_index("sec")
    ctx = lax.axis_index("ctx")
    ch = lax.axis_index("ch")
    has_before = ctx > 0
    has_after = ctx < n_ctx - 1

    def cut(index):
        return pl.ds(pl.multiple_of(index * width, width), width)

    mine = cut(sec)
    halves = [slice(low, low + LANES) for low in range(0, width, LANES)]
    loads = [
        pltpu.make_async_copy(inputs, x_ref, load_sem.at[0]),
        pltpu.make_async_copy(rates.at[:, mine], rate_ref, load_sem.at[1]),
        pltpu.make_async_copy(residues.at[:, mine], residue_ref, load_sem.at[2]),
        pltpu.make_async_copy(direct.at[:, mine], direct_ref, load_sem.at[3]),
        pltpu.make_async_copy(gain.at[:, mine], gain_ref, load_sem.at[4]),
        pltpu.make_async_copy(short.at[:, :, mine], short_ref, load_sem.at[5]),
        pltpu.make_async_copy(medium.at[:, mine], medium_ref, load_sem.at[6]),
        pltpu.make_async_copy(key.at[0, :, mine], key_ref.at[sec], key_recv.at[sec]),
        pltpu.make_async_copy(query.at[0, :, mine], query_ref.at[sec], query_recv.at[sec]),
        pltpu.make_async_copy(own_waves, own_ref, load_sem.at[7]),
        pltpu.make_async_copy(all_waves, all_ref, load_sem.at[8]),
        pltpu.make_async_copy(back_waves, back_ref, load_sem.at[9]),
    ]
    for load in loads:
        load.start()

    own = ch * sections + sec
    places = [(to_sec, to_ch) for to_ch in range(n_ch) for to_sec in range(sections)]

    def order(at_sec, at_ch):
        steps = at_sec % 2 + at_sec // 2 + at_ch
        return steps * len(places) + at_ch * sections + at_sec

    turn = order(sec, ch)
    earlier = [order(*place) < turn for place in places]
    later = [order(*place) > turn for place in places]
    level = [ch == to_ch for _, to_ch in places]

    def count(flags):
        return sum(flag.astype(jnp.int32) for flag in flags)

    def every(flags, act):
        for index, place in enumerate(places):

            @pl.when(flags[index])
            def _(index=index, place=place):
                act(index, *place)

    def signal(sem, device):
        pl.semaphore_signal(sem, inc=1, device_id=device, device_id_type=MESH)

    def await_all(sem, number):
        @pl.when(number > 0)
        def _():
            pl.semaphore_wait(sem, number)

    barrier = pltpu.get_barrier_semaphore()
    every(later, lambda _, *at: signal(barrier, {"sec": at[0], "ch": at[1]}))

    @pl.when(has_after)
    def _():
        signal(barrier, {"ctx": ctx + 1})

    await_all(barrier, count(earlier) + has_before.astype(jnp.int32))

    def greet(index, to_sec, to_ch):
        @pl.when(level[index])
        def _():
            signal(peer_sem.at[sec], {"sec": to_sec, "ch": to_ch})

        @pl.when(jnp.logical_not(level[index]))
        def _():
            signal(far_sem, {"sec": to_sec, "ch": to_ch})

    every(earlier, greet)

    @pl.when(has_before)
    def _():
        signal(ready_sem, {"ctx": ctx - 1})

    def remote(src, dst, send_sem, recv_sem, device):
        return pltpu.make_async_remote_copy(
            src_ref=src,
            dst_ref=dst,
            send_sem=send_sem,
            recv_sem=recv_sem,
            device_id=device,
            device_id_type=MESH,
        )

    def send_sum(index, to_sec, to_ch):
        slot = sums_ref.at[own]
        remote(slot, slot, sum_send, sum_recv, {"sec": to_sec, "ch": to_ch}).start()

    def send_field(tables, to_sec):
        field, held, send_sem, recv_sem = tables
        remote(
            field.at[0, :, cut(to_sec)], held.at[sec], send_sem, recv_sem.at[sec], {"sec": to_sec}
        ).start()

    before = [order(to_sec, ch) < turn for to_sec in range(sections)]
    behind = [order(to_sec, ch) > turn for to_sec in range(sections)]

    def send_fields(flags, tables):
        for to_sec, flag in reversed(list(enumerate(flags))):

            @pl.when(flag)
            def _(to_sec=to_sec):
                send_field(tables, to_sec)

    def both(first, second):
        return [jnp.logical_and(one, two) for one, two in zip(first, second)]

    keys = key, key_ref, key_send, key_recv
    queries = query, query_ref, query_send, query_recv
    far = [jnp.logical_not(flag) for flag in level]
    send_fields(before, keys)

    loads[0].wait()
    squares = jnp.square(x_ref[...].astype(F32))
    folded = sum(squares[:, low : low + LANES] for low in range(0, width, LANES))
    sums_ref[own] = jnp.sum(folded.T, axis=0, keepdims=True)

    every(earlier, send_sum)
    for to_sec in range(sections):

        @pl.when(behind[to_sec])
        def _(to_sec=to_sec):
            pl.semaphore_wait(peer_sem.at[to_sec], 1)
            send_sum(ch * sections + to_sec, to_sec, ch)
            send_field(keys, to_sec)

    send_fields([sec != to_sec for to_sec in range(sections)], queries)

    def arrived(ref, sem):
        pltpu.make_async_copy(ref, ref, sem).wait()

    for load in loads[1:7] + loads[9:]:
        load.wait()
    offsets = row_ids((length, width)).astype(F32)
    ages = (length - 1.0) - offsets
    rate_table = rate_ref[...]
    weights = residue_ref[...] * jnp.sqrt(1.0 - jnp.exp(-2.0 * rate_table))
    taps = jnp.where(row_ids((length, width)) == 0, direct_ref[...], 0.0)
    for mode in range(modes):
        rate = rate_table[mode : mode + 1]
        part = weights[mode : mode + 1] * jnp.exp(-rate * offsets)
        carry_ref[mode] = part
        age_ref[mode] = jnp.exp(-rate * ages)
        taps = taps + part
    first = row_ids((length, width)) == 0
    for index, filter_taps in enumerate((medium_ref[...], taps)):
        spectrum = times_parts(own_ref, filter_taps)
        real, imag = spectrum[:length], spectrum[length:]
        spectra_ref[index, 0] = real
        spectra_ref[index, 1] = jnp.where(first, 0.0, imag)
        spectra_ref[index, 2] = jnp.where(first, imag, real)

    scaled_ref[...] = x_ref[...].astype(F32) * gain_ref[...]

    @pl.when(jnp.logical_not(has_before))
    def _():
        padded_ref[:, :, :ROWS] = jnp.zeros((2, len(halves), ROWS, LANES), F32)

    await_all(far_sem, count(both(later, far)))
    every(both(later, far), send_sum)

    peers = len(places) - 1
    arrived(sums_ref.at[pl.ds(0, peers)], sum_recv)
    total = sums_ref[0]
    for index in range(1, len(places)):
        total = total + sums_ref[index]
    inverse = lax.rsqrt(total / (width * len(places)) + norm_eps)
    scale = jnp.broadcast_to(inverse, (length, length)).T
    for half in halves:
        stream_ref[:, half] = scaled_ref[:, half] * scale

    @pl.when(has_after)
    def _():
        pl.semaphore_wait(ready_sem, 1)

    after = {"ctx": lax.rem(ctx + 1, n_ctx)}

    def hand_over(section, src, dst):
        return remote(src, dst, ctx_send.at[section], ctx_recv.at[section], after)

    def gated(section):
        return key_ref[section].astype(F32) * stream_ref[...]

    def advance(section, filtered):
        arrived(query_ref.at[section], query_recv.at[section])
        return stream_ref[...] + query_ref[section].astype(F32) * filtered

    def short_section(section, tap_set):
        hand = hand_over(
            section,
            padded_ref.at[tap_set, :, pl.ds(length, ROWS)],
            padded_ref.at[tap_set, :, pl.ds(0, ROWS)],
        )
        values = gated(section)
        for index, half in enumerate(halves):
            padded_ref[tap_set, index, ROWS:] = values[:, half]

        @pl.when(has_after)
        def _():
            hand.start()

        @pl.when(has_before)
        def _():
            hand.wait_recv()

        filtered = []
        for index, half in enumerate(halves):
            taps = short_ref[:, tap_set, half]
            total = values[:, half] * taps[:1]
            for tap in range(1, taps.shape[0]):
                rows = padded_ref[tap_set, index, pl.ds(ROWS - tap, length)]
                total = total + rows * taps[tap : tap + 1]
            filtered.append(total)
        return hand, advance(section, jnp.concatenate(filtered, axis=1))

    def from_spectrum(index, spectrum):
        real, imag = spectrum[:length], spectrum[length:]
        first, cross, last = (spectra_ref[index, place] for place in range(3))
        product = jnp.concatenate(
            [real * first - imag * cross, real * cross + imag * last], axis=0
        )
        return times(back_ref[...], product)

    def medium_section(section):
        hand = hand_over(section, gated_ref, rows_ref)
        gated_ref[...] = gated(section).astype(BF16)

        @pl.when(has_after)
        def _():
            hand.start()

        arrived(query_ref.at[section], query_recv.at[section])

        def finish(spectrum):
            filtered = from_spectrum(0, spectrum)
            stream_ref[...] += query_ref[section].astype(F32) * filtered

        @pl.when(jnp.logical_not(has_before))
        def _():
            finish(times(own_ref[0], gated_ref[...]))

        @pl.when(has_before)
        def _():
            hand.wait_recv()
            both = jnp.concatenate([gated_ref[...], rows_ref[...]], axis=0)
            finish(times(all_ref[...], both))

        return hand

    def long_section(section):
        hand = hand_over(section, leaving_ref, state_ref)
        values = gated(section)
        arrived(query_ref.at[section], query_recv.at[section])

        def leave():
            for mode in range(modes):
                leaving_ref[mode : mode + 1] = jnp.sum(
                    age_ref[mode] * values, axis=0, keepdims=True
                )

        @pl.when(jnp.logical_not(has_before))
        def _():
            spectrum = times(own_ref[0], values)
            if n_ctx > 1:
                leave()
                hand.start()
            filtered = from_spectrum(1, spectrum)
            stream_ref[...] += query_ref[section].astype(F32) * filtered

        @pl.when(has_before)
        def _():
            spectrum = times(own_ref[0], values)

            @pl.when(has_after)
            def _():
                leave()

            hand.wait_recv()

            @pl.when(has_after)
            def _():
                leaving_ref[...] += jnp.exp(-length * rate_ref[...]) * state_ref[...]
                hand.start()

            entering = jnp.exp(-rate_ref[...]) * state_ref[...]
            filtered = from_spectrum(1, spectrum)
            for mode in range(modes):
                filtered = filtered + carry_ref[mode] * entering[mode : mode + 1]
            stream_ref[...] += query_ref[section].astype(F32) * filtered

        return hand

    hands = []
    for section in range(sections):
        arrived(key_ref.at[section], key_recv.at[section])
        if section == 1:
            hands.append(medium_section(section))
        elif section == 2:
            hands.append(long_section(section))
        else:
            hand, stream = short_section(section, min(section, 1))
            hands.append(hand)
            if section:
                out[...] = stream.astype(BF16)
            else:
                stream_ref[...] = stream

    arrived(sums_ref.at[pl.ds(0, peers)], sum_send)
    arrived(key_ref.at[pl.ds(0, sections - 1)], key_send)
    arrived(query_ref.at[pl.ds(0, sections - 1)], query_send)

    @pl.when(has_after)
    def _():
        for hand in hands:
            hand.wait_send()


def shards(
    inputs,
    query_fields,
    key_fields,
    norm_gain,
    short_taps,
    medium_taps,
    pole_rates,
    pole_residues,
    direct_term,
):
    sections = lax.axis_size("sec")
    n_ctx = lax.axis_size("ctx")
    n_ch = lax.axis_size("ch")
    length, width = inputs.shape
    modes = pole_rates.shape[0]
    shorts, short_span = short_taps.shape[:2]
    tables = waves(length)
    anywhere = pl.BlockSpec(memory_space=pl.ANY)
    dma = pltpu.SemaphoreType.DMA
    return pl.pallas_call(
        functools.partial(kernel, sections, n_ctx, n_ch),
        out_shape=jax.ShapeDtypeStruct((length, width), inputs.dtype),
        in_specs=[anywhere] * 12,
        out_specs=pl.BlockSpec(memory_space=pltpu.VMEM),
        scratch_shapes=[
            pltpu.VMEM((length, width), inputs.dtype),
            pltpu.VMEM((1, width), F32),
            pltpu.VMEM((short_span, shorts, width), F32),
            pltpu.VMEM((medium_taps.shape[0], width), F32),
            pltpu.VMEM((modes, width), F32),
            pltpu.VMEM((modes, width), F32),
            pltpu.VMEM((1, width), F32),
            pltpu.VMEM((sections, length, width), key_fields.dtype),
            pltpu.VMEM((sections, length, width), query_fields.dtype),
            pltpu.VMEM((n_ch * sections, 1, length), F32),
            pltpu.VMEM((2, width // LANES, ROWS + length, LANES), F32),
            pltpu.VMEM((length, width), BF16),
            pltpu.VMEM((length, width), BF16),
            pltpu.VMEM((length, width), F32),
            pltpu.VMEM((length, width), F32),
            pltpu.VMEM((modes, width), F32),
            pltpu.VMEM((modes, width), F32),
            pltpu.VMEM((modes, length, width), F32),
            pltpu.VMEM((modes, length, width), F32),
            pltpu.VMEM(tables[0].shape, BF16),
            pltpu.VMEM(tables[1].shape, BF16),
            pltpu.VMEM(tables[2].shape, BF16),
            pltpu.VMEM((2, 3, length, width), F32),
            dma((10,)),
            dma,
            dma((sections,)),
            dma,
            dma((sections,)),
            dma,
            dma,
            dma((sections,)),
            dma((sections,)),
            pltpu.SemaphoreType.REGULAR((sections,)),
            pltpu.SemaphoreType.REGULAR,
            pltpu.SemaphoreType.REGULAR,
        ],
        compiler_params=pltpu.CompilerParams(collective_id=0, has_side_effects=True, vmem_limit_bytes=8*2**20),
    )(*[pltpu.with_memory_space_constraint(a, pltpu.HBM) for a in (
        inputs,
        query_fields,
        key_fields,
        norm_gain[None],
        jnp.swapaxes(short_taps, 0, 1),
        medium_taps,
        pole_rates,
        pole_residues,
        direct_term[None],
        *(jnp.asarray(table) for table in tables),
    )])


def solution(mesh):
    in_specs = (
        P("ctx", ("ch", "sec")),
        P("sec", "ctx", "ch"),
        P("sec", "ctx", "ch"),
        P("ch"),
        P(None, None, "ch"),
        P(None, "ch"),
        P(None, "ch"),
        P(None, "ch"),
        P("ch"),
    )
    out_specs = P("ctx", ("ch", "sec"))
    return jax.shard_map(shards, mesh=mesh, in_specs=in_specs, out_specs=out_specs, check_vma=False)
```

time: 15.1 us -> 13.3 us (0.88)
  the two profiles are of different devices: /device:TPU:9 before, /device:TPU:19 now
where the time goes in v3:
time: 13.3 us; the launch traced here: 13.2 us
  Pallas kernels  12.6 us (95%)
  local copies, waits for them, and re-layouts  0.63 us (5%)
    pallas_call x1, Pallas kernels, shards(): pl.pallas_call(functools.partial(kernel, sections, n_ctx, n_ch), out_shap...  12.6 us
    unnamed x1, local copies, waits for them, and re-layouts  0.63 us

profile of v3, /device:TPU:19, one launch (start us, length us, event | category | flops | bytes accessed | tf_op | source)
XLA Modules:
  0.0 13.2 jit_solution(7633275268554129247)
XLA Ops:
  0.0 12.6 %shard_map.118 = bf16[128,256]{1,0:T(8,128)(2,1)S(1)} custom-call(bf16[128,256]{1,0:T(8,128)(2,1)} %inputs.1, bf16[1,128,1024]{2,1,0:T(8,128)(2,1)} %query.1, bf16[1,128,1024]{2,1,0:T(8,128)(2,1)} %key.1, f32[1,1024]{1,0:T(1,128)} %bitcast.4, f32[7,2,1024]{2,1,0:T(2,128)} %bitcast.3, f32[128,1024]{1,0:T(8,128)} %medium.1, f32[8,1024]{1,0:T(8,128)} %rates.1, ...), custom_call_target="tpu_custom_call" | custom-call | tf_op jit(solution)/shard_map/pallas_call | solution.py:455
  12.6 0.6 %copy.14 = bf16[128,256]{1,0:T(8,128)(2,1)} copy(bf16[128,256]{1,0:T(8,128)(2,1)S(1)} %shard_map.118) | data formatting | bytes 131072

commit v4 on v3

--- a/solution.py
+++ b/solution.py
@@ -136,58 +136,44 @@
         load.start()
 
     own = ch * sections + sec
-    places = [(to_sec, to_ch) for to_ch in range(n_ch) for to_sec in range(sections)]
-
-    def order(at_sec, at_ch):
-        steps = at_sec % 2 + at_sec // 2 + at_ch
-        return steps * len(places) + at_ch * sections + at_sec
-
-    turn = order(sec, ch)
-    earlier = [order(*place) < turn for place in places]
-    later = [order(*place) > turn for place in places]
-    level = [ch == to_ch for _, to_ch in places]
-
-    def count(flags):
-        return sum(flag.astype(jnp.int32) for flag in flags)
-
-    def every(flags, act):
-        for index, place in enumerate(places):
-
-            @pl.when(flags[index])
-            def _(index=index, place=place):
-                act(index, *place)
-
-    def signal(sem, device):
-        pl.semaphore_signal(sem, inc=1, device_id=device, device_id_type=MESH)
-
-    def await_all(sem, number):
-        @pl.when(number > 0)
-        def _():
-            pl.semaphore_wait(sem, number)
+    members = range(sections)
+    places = [(to_sec, to_ch) for to_ch in range(n_ch) for to_sec in members]
+    last, top = sections - 1, n_ch - 1
+    opens, closes = sec == 0, sec == last
+    middle = jnp.logical_not(jnp.logical_or(opens, closes))
+    corner = jnp.logical_and(closes, ch == top)
+
+    def also(one, two):
+        return jnp.logical_and(one, two)
+
+    def signal(flag, sem, device):
+        @pl.when(flag)
+        def _():
+            pl.semaphore_signal(sem, inc=1, device_id=device, device_id_type=MESH)
 
     barrier = pltpu.get_barrier_semaphore()
-    every(later, lambda _, *at: signal(barrier, {"sec": at[0], "ch": at[1]}))
-
-    @pl.when(has_after)
+    signal(middle, barrier, {"sec": last})
+    for to_sec in members[1:]:
+        signal(opens, barrier, {"sec": to_sec})
+    signal(ch < top, barrier, {"sec": last, "ch": top})
+    signal(has_after, barrier, {"ctx": ctx + 1})
+    heard = (
+        middle.astype(jnp.int32)
+        + closes.astype(jnp.int32) * last
+        + corner.astype(jnp.int32) * (sections * top)
+        + has_before.astype(jnp.int32)
+    )
+
+    @pl.when(heard > 0)
     def _():
-        signal(barrier, {"ctx": ctx + 1})
-
-    await_all(barrier, count(earlier) + has_before.astype(jnp.int32))
-
-    def greet(index, to_sec, to_ch):
-        @pl.when(level[index])
-        def _():
-            signal(peer_sem.at[sec], {"sec": to_sec, "ch": to_ch})
-
-        @pl.when(jnp.logical_not(level[index]))
-        def _():
-            signal(far_sem, {"sec": to_sec, "ch": to_ch})
-
-    every(earlier, greet)
-
-    @pl.when(has_before)
-    def _():
-        signal(ready_sem, {"ctx": ctx - 1})
+        pl.semaphore_wait(barrier, heard)
+
+    for to_sec in members[:-1]:
+        signal(closes, peer_sem.at[last], {"sec": to_sec})
+    signal(middle, peer_sem.at[sec], {"sec": 0})
+    for to_sec, to_ch in places[:-1]:
+        signal(corner, far_sem, {"sec": to_sec, "ch": to_ch})
+    signal(has_before, ready_sem, {"ctx": ctx - 1})
 
     def remote(src, dst, send_sem, recv_sem, device):
         return pltpu.make_async_remote_copy(
@@ -199,7 +185,7 @@
             device_id_type=MESH,
         )
 
-    def send_sum(index, to_sec, to_ch):
+    def send_sum(to_sec, to_ch):
         slot = sums_ref.at[own]
         remote(slot, slot, sum_send, sum_recv, {"sec": to_sec, "ch": to_ch}).start()
 
@@ -209,39 +195,57 @@
             field.at[0, :, cut(to_sec)], held.at[sec], send_sem, recv_sem.at[sec], {"sec": to_sec}
         ).start()
 
-    before = [order(to_sec, ch) < turn for to_sec in range(sections)]
-    behind = [order(to_sec, ch) > turn for to_sec in range(sections)]
-
-    def send_fields(flags, tables):
-        for to_sec, flag in reversed(list(enumerate(flags))):
-
-            @pl.when(flag)
-            def _(to_sec=to_sec):
-                send_field(tables, to_sec)
-
-    def both(first, second):
-        return [jnp.logical_and(one, two) for one, two in zip(first, second)]
+    def send_far():
+        for to_sec, to_ch in places:
+
+            @pl.when(ch != to_ch)
+            def _(to_sec=to_sec, to_ch=to_ch):
+                send_sum(to_sec, to_ch)
+
+    def each(flag, chosen, act):
+        @pl.when(flag)
+        def _():
+            for to_sec in chosen:
+                act(to_sec)
 
     keys = key, key_ref, key_send, key_recv
     queries = query, query_ref, query_send, query_recv
-    far = [jnp.logical_not(flag) for flag in level]
-    send_fields(before, keys)
+    each(middle, members[:1], lambda to_sec: send_field(keys, to_sec))
+    each(closes, members[:-1], lambda to_sec: send_field(keys, to_sec))
 
     loads[0].wait()
     squares = jnp.square(x_ref[...].astype(F32))
     folded = sum(squares[:, low : low + LANES] for low in range(0, width, LANES))
     sums_ref[own] = jnp.sum(folded.T, axis=0, keepdims=True)
 
-    every(earlier, send_sum)
-    for to_sec in range(sections):
-
-        @pl.when(behind[to_sec])
-        def _(to_sec=to_sec):
-            pl.semaphore_wait(peer_sem.at[to_sec], 1)
-            send_sum(ch * sections + to_sec, to_sec, ch)
-            send_field(keys, to_sec)
-
-    send_fields([sec != to_sec for to_sec in range(sections)], queries)
+    pl.when(corner)(send_far)
+    each(middle, members[:1], lambda to_sec: send_sum(to_sec, ch))
+    each(closes, members[:-1], lambda to_sec: send_sum(to_sec, ch))
+
+    def meet(to_sec):
+        pl.semaphore_wait(peer_sem.at[to_sec], 1)
+        send_sum(to_sec, ch)
+        send_field(keys, to_sec)
+
+    each(opens, members[1:], meet)
+
+    @pl.when(middle)
+    def _():
+        pl.semaphore_wait(peer_sem.at[last], 1)
+
+    for act in (lambda to_sec: send_sum(to_sec, ch), lambda to_sec: send_field(keys, to_sec)):
+        for to_sec in members[1:]:
+            each(also(middle, sec != to_sec), [to_sec], act)
+    for to_sec in members:
+        each(sec != to_sec, [to_sec], lambda to_sec: send_field(queries, to_sec))
+
+    def far_sums():
+        pl.semaphore_wait(far_sem, 1)
+        send_far()
+
+    steps = sec % 2 + sec // 2 + ch
+    late = 2 * steps > last % 2 + last // 2 + top
+    pl.when(also(late, jnp.logical_not(corner)))(far_sums)
 
     def arrived(ref, sem):
         pltpu.make_async_copy(ref, ref, sem).wait()
@@ -273,8 +277,7 @@
     def _():
         padded_ref[:, :, :ROWS] = jnp.zeros((2, len(halves), ROWS, LANES), F32)
 
-    await_all(far_sem, count(both(later, far)))
-    every(both(later, far), send_sum)
+    pl.when(jnp.logical_not(late))(far_sums)
 
     peers = len(places) - 1
     arrived(sums_ref.at[pl.ds(0, peers)], sum_recv)

time: 13.3 us -> 12.8 us (0.962)
  the two profiles are of different devices: /device:TPU:19 before, /device:TPU:1 now
where the time goes in v4:
time: 12.8 us; the launch traced here: 12.6 us
  Pallas kernels  12 us (94%)
  local copies, waits for them, and re-layouts  0.63 us (5%)
    pallas_call x1, Pallas kernels, shards(): pl.pallas_call(functools.partial(kernel, sections, n_ctx, n_ch), out_shap...  12 us
    unnamed x1, local copies, waits for them, and re-layouts  0.63 us

profile of v4, /device:TPU:1, one launch (start us, length us, event | category | flops | bytes accessed | tf_op | source)
XLA Modules:
  0.0 12.6 jit_solution(73922555536022308)
XLA Ops:
  0.0 12.0 %shard_map.118 = bf16[128,256]{1,0:T(8,128)(2,1)S(1)} custom-call(bf16[128,256]{1,0:T(8,128)(2,1)} %inputs.1, bf16[1,128,1024]{2,1,0:T(8,128)(2,1)} %query.1, bf16[1,128,1024]{2,1,0:T(8,128)(2,1)} %key.1, f32[1,1024]{1,0:T(1,128)} %bitcast.4, f32[7,2,1024]{2,1,0:T(2,128)} %bitcast.3, f32[128,1024]{1,0:T(8,128)} %medium.1, f32[8,1024]{1,0:T(8,128)} %rates.1, ...), custom_call_target="tpu_custom_call" | custom-call | tf_op jit(solution)/shard_map/pallas_call | solution.py:458
  12.0 0.6 %copy.14 = bf16[128,256]{1,0:T(8,128)(2,1)} copy(bf16[128,256]{1,0:T(8,128)(2,1)S(1)} %shard_map.118) | data formatting | bytes 131072

commit v5 on v4

--- a/solution.py
+++ b/solution.py
@@ -26,7 +26,15 @@
 
 
 def times(table, values):
-    return jnp.dot(table, values.astype(BF16), preferred_element_type=F32)
+    values = values.astype(BF16)
+    half = table.shape[0] // 2
+    return jnp.concatenate(
+        [
+            jnp.dot(rows, values, preferred_element_type=F32)
+            for rows in (table[:half], table[half:])
+        ],
+        axis=0,
+    )
 
 
 def times_parts(table, values):
@@ -84,10 +92,14 @@
     rows_ref,
     scaled_ref,
     stream_ref,
+    waiting_ref,
     state_ref,
     leaving_ref,
     age_ref,
     carry_ref,
+    decay_ref,
+    ending_ref,
+    within_ref,
     own_ref,
     all_ref,
     back_ref,
@@ -104,6 +116,7 @@
     peer_sem,
     far_sem,
     ready_sem,
+    turn_sem,
 ):
     length, width = x_ref.shape
     modes = rate_ref.shape[0]
@@ -208,6 +221,8 @@
             for to_sec in chosen:
                 act(to_sec)
 
+    leads, follows = ctx % 2 == 0, ctx % 2 == 1
+    led = also(leads, has_after)
     keys = key, key_ref, key_send, key_recv
     queries = query, query_ref, query_send, query_recv
     each(middle, members[:1], lambda to_sec: send_field(keys, to_sec))
@@ -236,8 +251,12 @@
     for act in (lambda to_sec: send_sum(to_sec, ch), lambda to_sec: send_field(keys, to_sec)):
         for to_sec in members[1:]:
             each(also(middle, sec != to_sec), [to_sec], act)
-    for to_sec in members:
-        each(sec != to_sec, [to_sec], lambda to_sec: send_field(queries, to_sec))
+    def send_queries():
+        each(opens, members[:0:-1], lambda to_sec: send_field(queries, to_sec))
+        for to_sec in members:
+            each(also(jnp.logical_not(opens), sec != to_sec), [to_sec], lambda to_sec: send_field(queries, to_sec))
+
+    pl.when(leads)(send_queries)
 
     def far_sums():
         pl.semaphore_wait(far_sem, 1)
@@ -263,6 +282,20 @@
         carry_ref[mode] = part
         age_ref[mode] = jnp.exp(-rate * ages)
         taps = taps + part
+    decay_ref[0] = jnp.exp(-rate_table)
+    decay_ref[1] = jnp.exp(-length * rate_table)
+    edge = row_ids((ROWS, width))
+    for mode in range(modes):
+        rate = rate_table[mode : mode + 1]
+        ending_ref[mode] = weights[mode : mode + 1] * jnp.exp(rate * (ROWS - 1.0 - edge.astype(F32)))
+    for row in range(ROWS):
+        ahead = (row - edge).astype(F32)
+        undone = jnp.where(edge == row, direct_ref[...], 0.0)
+        for mode in range(modes):
+            rate = rate_table[mode : mode + 1]
+            gone = weights[mode : mode + 1] * jnp.exp(rate * jnp.maximum(ahead, 0.0))
+            undone = undone - jnp.where(ahead > 0, gone, 0.0)
+        within_ref[row] = undone
     first = row_ids((length, width)) == 0
     for index, filter_taps in enumerate((medium_ref[...], taps)):
         spectrum = times_parts(own_ref, filter_taps)
@@ -278,6 +311,18 @@
         padded_ref[:, :, :ROWS] = jnp.zeros((2, len(halves), ROWS, LANES), F32)
 
     pl.when(jnp.logical_not(late))(far_sums)
+
+    @pl.when(led)
+    def _():
+        pl.semaphore_wait(ready_sem, 1)
+        arrived(key_ref.at[pl.ds(0, sections - 1)], key_send)
+        pl.semaphore_signal(turn_sem, inc=1, device_id={"ctx": ctx + 1}, device_id_type=MESH)
+
+    @pl.when(follows)
+    def _():
+        pl.semaphore_wait(turn_sem, 1)
+        send_queries()
+
 
     peers = len(places) - 1
     arrived(sums_ref.at[pl.ds(0, peers)], sum_recv)
@@ -289,7 +334,7 @@
     for half in halves:
         stream_ref[:, half] = scaled_ref[:, half] * scale
 
-    @pl.when(has_after)
+    @pl.when(also(follows, has_after))
     def _():
         pl.semaphore_wait(ready_sem, 1)
 
@@ -306,22 +351,31 @@
         return stream_ref[...] + query_ref[section].astype(F32) * filtered
 
     def short_section(section, tap_set):
-        hand = hand_over(
-            section,
-            padded_ref.at[tap_set, :, pl.ds(length, ROWS)],
-            padded_ref.at[tap_set, :, pl.ds(0, ROWS)],
-        )
         values = gated(section)
         for index, half in enumerate(halves):
             padded_ref[tap_set, index, ROWS:] = values[:, half]
-
-        @pl.when(has_after)
-        def _():
-            hand.start()
-
-        @pl.when(has_before)
-        def _():
-            hand.wait_recv()
+        hand = None
+        if tap_set:
+
+            @pl.when(has_before)
+            def _():
+                for index, half in enumerate(halves):
+                    padded_ref[tap_set, index, :ROWS] = state_ref[modes:, half]
+
+        else:
+            hand = hand_over(
+                section,
+                padded_ref.at[tap_set, :, pl.ds(length, ROWS)],
+                padded_ref.at[tap_set, :, pl.ds(0, ROWS)],
+            )
+
+            @pl.when(has_after)
+            def _():
+                hand.start()
+
+            @pl.when(has_before)
+            def _():
+                hand.wait_recv()
 
         filtered = []
         for index, half in enumerate(halves):
@@ -372,61 +426,83 @@
         values = gated(section)
         arrived(query_ref.at[section], query_recv.at[section])
 
+        arrived(key_ref.at[section + 1], key_recv.at[section + 1])
+        end = pl.ds(length - ROWS, ROWS)
+
         def leave():
             for mode in range(modes):
                 leaving_ref[mode : mode + 1] = jnp.sum(
                     age_ref[mode] * values, axis=0, keepdims=True
                 )
 
+        def send_end():
+            states = leaving_ref[:modes]
+            rows = values[length - ROWS :]
+            filtered = ending_ref[0] * states[:1]
+            for mode in range(1, modes):
+                filtered = filtered + ending_ref[mode] * states[mode : mode + 1]
+            for row in range(ROWS):
+                filtered = filtered + within_ref[row] * rows[row : row + 1]
+            stream = stream_ref[end] + query_ref[section, end].astype(F32) * filtered
+            leaving_ref[modes:] = key_ref[section + 1, end].astype(F32) * stream
+            hand.start()
+
         @pl.when(jnp.logical_not(has_before))
         def _():
             spectrum = times(own_ref[0], values)
             if n_ctx > 1:
                 leave()
-                hand.start()
+                send_end()
             filtered = from_spectrum(1, spectrum)
             stream_ref[...] += query_ref[section].astype(F32) * filtered
 
         @pl.when(has_before)
         def _():
-            spectrum = times(own_ref[0], values)
+            filtered = from_spectrum(1, times(own_ref[0], values))
+            waiting_ref[...] = stream_ref[...] + query_ref[section].astype(F32) * filtered
 
             @pl.when(has_after)
             def _():
                 leave()
 
             hand.wait_recv()
+            states = state_ref[:modes]
 
             @pl.when(has_after)
             def _():
-                leaving_ref[...] += jnp.exp(-length * rate_ref[...]) * state_ref[...]
-                hand.start()
-
-            entering = jnp.exp(-rate_ref[...]) * state_ref[...]
-            filtered = from_spectrum(1, spectrum)
-            for mode in range(modes):
-                filtered = filtered + carry_ref[mode] * entering[mode : mode + 1]
-            stream_ref[...] += query_ref[section].astype(F32) * filtered
+                leaving_ref[:modes] += decay_ref[1] * states
+                send_end()
+
+            entering = decay_ref[0] * states
+            carried = carry_ref[0] * entering[:1]
+            for mode in range(1, modes):
+                carried = carried + carry_ref[mode] * entering[mode : mode + 1]
+            stream_ref[...] = waiting_ref[...] + query_ref[section].astype(F32) * carried
 
         return hand
 
     hands = []
     for section in range(sections):
-        arrived(key_ref.at[section], key_recv.at[section])
+        if section < sections - 1:
+            arrived(key_ref.at[section], key_recv.at[section])
         if section == 1:
             hands.append(medium_section(section))
         elif section == 2:
             hands.append(long_section(section))
         else:
             hand, stream = short_section(section, min(section, 1))
-            hands.append(hand)
             if section:
                 out[...] = stream.astype(BF16)
             else:
+                hands.append(hand)
                 stream_ref[...] = stream
 
     arrived(sums_ref.at[pl.ds(0, peers)], sum_send)
-    arrived(key_ref.at[pl.ds(0, sections - 1)], key_send)
+
+    @pl.when(jnp.logical_not(led))
+    def _():
+        arrived(key_ref.at[pl.ds(0, sections - 1)], key_send)
+
     arrived(query_ref.at[pl.ds(0, sections - 1)], query_send)
 
     @pl.when(has_after)
@@ -476,10 +552,14 @@
             pltpu.VMEM((length, width), BF16),
             pltpu.VMEM((length, width), F32),
             pltpu.VMEM((length, width), F32),
-            pltpu.VMEM((modes, width), F32),
-            pltpu.VMEM((modes, width), F32),
+            pltpu.VMEM((length, width), F32),
+            pltpu.VMEM((modes + ROWS, width), F32),
+            pltpu.VMEM((modes + ROWS, width), F32),
             pltpu.VMEM((modes, length, width), F32),
             pltpu.VMEM((modes, length, width), F32),
+            pltpu.VMEM((2, modes, width), F32),
+            pltpu.VMEM((modes, ROWS, width), F32),
+            pltpu.VMEM((ROWS, ROWS, width), F32),
             pltpu.VMEM(tables[0].shape, BF16),
             pltpu.VMEM(tables[1].shape, BF16),
             pltpu.VMEM(tables[2].shape, BF16),
@@ -496,6 +576,7 @@
             pltpu.SemaphoreType.REGULAR((sections,)),
             pltpu.SemaphoreType.REGULAR,
             pltpu.SemaphoreType.REGULAR,
+            pltpu.SemaphoreType.REGULAR,
         ],
         compiler_params=pltpu.CompilerParams(collective_id=0, has_side_effects=True, vmem_limit_bytes=8*2**20),
     )(*[pltpu.with_memory_space_constraint(a, pltpu.HBM) for a in (

time: 12.8 us -> 12.7 us (level)
  no operation moved by 1% of the time
where the time goes in v5:
time: 12.7 us; the launch traced here: 12.5 us
  Pallas kernels  11.9 us (94%)
  local copies, waits for them, and re-layouts  0.63 us (5%)
    pallas_call x1, Pallas kernels, shards(): pl.pallas_call(functools.partial(kernel, sections, n_ctx, n_ch), out_shap...  11.9 us
    unnamed x1, local copies, waits for them, and re-layouts  0.63 us

profile of v5, /device:TPU:1, one launch (start us, length us, event | category | flops | bytes accessed | tf_op | source)
XLA Modules:
  0.0 12.5 jit_solution(9837942494142186)
XLA Ops:
  0.0 11.9 %shard_map.118 = bf16[128,256]{1,0:T(8,128)(2,1)S(1)} custom-call(bf16[128,256]{1,0:T(8,128)(2,1)} %inputs.1, bf16[1,128,1024]{2,1,0:T(8,128)(2,1)} %query.1, bf16[1,128,1024]{2,1,0:T(8,128)(2,1)} %key.1, f32[1,1024]{1,0:T(1,128)} %bitcast.4, f32[7,2,1024]{2,1,0:T(2,128)} %bitcast.3, f32[128,1024]{1,0:T(8,128)} %medium.1, f32[8,1024]{1,0:T(8,128)} %rates.1, ...), custom_call_target="tpu_custom_call" | custom-call | tf_op jit(solution)/shard_map/pallas_call | solution.py:534
  11.9 0.6 %copy.14 = bf16[128,256]{1,0:T(8,128)(2,1)} copy(bf16[128,256]{1,0:T(8,128)(2,1)S(1)} %shard_map.118) | data formatting | bytes 131072

commit v6 on v5

--- a/solution.py
+++ b/solution.py
@@ -92,6 +92,7 @@
     rows_ref,
     scaled_ref,
     stream_ref,
+    keyed_ref,
     waiting_ref,
     state_ref,
     leaving_ref,
@@ -324,14 +325,18 @@
         send_queries()
 
 
+    arrived(key_ref.at[0], key_recv.at[0])
+    keyed_ref[...] = scaled_ref[...] * key_ref[0].astype(F32)
     peers = len(places) - 1
     arrived(sums_ref.at[pl.ds(0, peers)], sum_recv)
-    total = sums_ref[0]
-    for index in range(1, len(places)):
-        total = total + sums_ref[index]
-    inverse = lax.rsqrt(total / (width * len(places)) + norm_eps)
+    totals = [sums_ref[index] for index in range(len(places))]
+    while len(totals) > 1:
+        odd = totals[len(totals) // 2 * 2 :]
+        totals = [one + two for one, two in zip(totals[::2], totals[1::2])] + odd
+    inverse = lax.rsqrt(totals[0] / (width * len(places)) + norm_eps)
     scale = jnp.broadcast_to(inverse, (length, length)).T
-    for half in halves:
+    for index, half in enumerate(halves):
+        padded_ref[0, index, ROWS:] = keyed_ref[:, half] * scale
         stream_ref[:, half] = scaled_ref[:, half] * scale
 
     @pl.when(also(follows, has_after))
@@ -351,11 +356,11 @@
         return stream_ref[...] + query_ref[section].astype(F32) * filtered
 
     def short_section(section, tap_set):
-        values = gated(section)
-        for index, half in enumerate(halves):
-            padded_ref[tap_set, index, ROWS:] = values[:, half]
         hand = None
         if tap_set:
+            values = gated(section)
+            for index, half in enumerate(halves):
+                padded_ref[tap_set, index, ROWS:] = values[:, half]
 
             @pl.when(has_before)
             def _():
@@ -380,7 +385,7 @@
         filtered = []
         for index, half in enumerate(halves):
             taps = short_ref[:, tap_set, half]
-            total = values[:, half] * taps[:1]
+            total = padded_ref[tap_set, index, pl.ds(ROWS, length)] * taps[:1]
             for tap in range(1, taps.shape[0]):
                 rows = padded_ref[tap_set, index, pl.ds(ROWS - tap, length)]
                 total = total + rows * taps[tap : tap + 1]
@@ -483,7 +488,7 @@
 
     hands = []
     for section in range(sections):
-        if section < sections - 1:
+        if 0 < section < sections - 1:
             arrived(key_ref.at[section], key_recv.at[section])
         if section == 1:
             hands.append(medium_section(section))
@@ -553,6 +558,7 @@
             pltpu.VMEM((length, width), F32),
             pltpu.VMEM((length, width), F32),
             pltpu.VMEM((length, width), F32),
+            pltpu.VMEM((length, width), F32),
             pltpu.VMEM((modes + ROWS, width), F32),
             pltpu.VMEM((modes + ROWS, width), F32),
             pltpu.VMEM((modes, length, width), F32),

time: 12.7 us -> 12.6 us (level)
  no operation moved by 1% of the time
where the time goes in v6:
time: 12.6 us; the launch traced here: 12.5 us
  Pallas kernels  11.8 us (94%)
  local copies, waits for them, and re-layouts  0.63 us (5%)
    pallas_call x1, Pallas kernels, shards(): pl.pallas_call(functools.partial(kernel, sections, n_ctx, n_ch), out_shap...  11.8 us
    unnamed x1, local copies, waits for them, and re-layouts  0.63 us

profile of v6, /device:TPU:1, one launch (start us, length us, event | category | flops | bytes accessed | tf_op | source)
XLA Modules:
  0.0 12.5 jit_solution(1167890579265789624)
XLA Ops:
  0.0 11.8 %shard_map.118 = bf16[128,256]{1,0:T(8,128)(2,1)S(1)} custom-call(bf16[128,256]{1,0:T(8,128)(2,1)} %inputs.1, bf16[1,128,1024]{2,1,0:T(8,128)(2,1)} %query.1, bf16[1,128,1024]{2,1,0:T(8,128)(2,1)} %key.1, f32[1,1024]{1,0:T(1,128)} %bitcast.4, f32[7,2,1024]{2,1,0:T(2,128)} %bitcast.3, f32[128,1024]{1,0:T(8,128)} %medium.1, f32[8,1024]{1,0:T(8,128)} %rates.1, ...), custom_call_target="tpu_custom_call" | custom-call | tf_op jit(solution)/shard_map/pallas_call | solution.py:539
  11.9 0.6 %copy.14 = bf16[128,256]{1,0:T(8,128)(2,1)} copy(bf16[128,256]{1,0:T(8,128)(2,1)S(1)} %shard_map.118) | data formatting | bytes 131072

commit v7 on v5

--- a/solution.py
+++ b/solution.py
@@ -461,17 +461,18 @@
             filtered = from_spectrum(1, times(own_ref[0], values))
             waiting_ref[...] = stream_ref[...] + query_ref[section].astype(F32) * filtered
 
-            @pl.when(has_after)
-            def _():
-                leave()
+            if n_ctx > 2:
+                pl.when(has_after)(leave)
 
             hand.wait_recv()
             states = state_ref[:modes]
 
-            @pl.when(has_after)
-            def _():
-                leaving_ref[:modes] += decay_ref[1] * states
-                send_end()
+            if n_ctx > 2:
+
+                @pl.when(has_after)
+                def _():
+                    leaving_ref[:modes] += decay_ref[1] * states
+                    send_end()
 
             entering = decay_ref[0] * states
             carried = carry_ref[0] * entering[:1]

time: 12.7 us -> 12.7 us (level)
  no operation moved by 1% of the time
where the time goes in v7:
time: 12.7 us; the launch traced here: 12.5 us
  Pallas kernels  11.9 us (94%)
  local copies, waits for them, and re-layouts  0.63 us (5%)
    pallas_call x1, Pallas kernels, shards(): pl.pallas_call(functools.partial(kernel, sections, n_ctx, n_ch), out_shap...  11.9 us
    unnamed x1, local copies, waits for them, and re-layouts  0.63 us

profile of v7, /device:TPU:1, one launch (start us, length us, event | category | flops | bytes accessed | tf_op | source)
XLA Modules:
  0.0 12.5 jit_solution(13843822982302415839)
XLA Ops:
  0.0 11.9 %shard_map.118 = bf16[128,256]{1,0:T(8,128)(2,1)S(1)} custom-call(bf16[128,256]{1,0:T(8,128)(2,1)} %inputs.1, bf16[1,128,1024]{2,1,0:T(8,128)(2,1)} %query.1, bf16[1,128,1024]{2,1,0:T(8,128)(2,1)} %key.1, f32[1,1024]{1,0:T(1,128)} %bitcast.4, f32[7,2,1024]{2,1,0:T(2,128)} %bitcast.3, f32[128,1024]{1,0:T(8,128)} %medium.1, f32[8,1024]{1,0:T(8,128)} %rates.1, ...), custom_call_target="tpu_custom_call" | custom-call | tf_op jit(solution)/shard_map/pallas_call | solution.py:535
  11.9 0.6 %copy.14 = bf16[128,256]{1,0:T(8,128)(2,1)} copy(bf16[128,256]{1,0:T(8,128)(2,1)S(1)} %shard_map.118) | data formatting | bytes 131072
